TPU v7x, 32 devices: a whole 2x2x4 slice. The times are simulated.
32 devices in a mesh: head: 4 (over x, core), tok: 8 (over z, y).
Axes of the slice: x: 2, y: 2, z: 4, core: 2. Of those that a mesh axis runs over, the one named last changes fastest.
Arguments:
- tokens: bfloat16 [512, 4096], P('tok'), may hold values from -6 to 6
- attn_gain: float32 [4096], replicated, may hold values from 0.5 to 1.5
- q_weight: bfloat16 [4096, 2048], P('tok', 'head'), may hold values from -0.09375 to 0.09375
- k_weight: bfloat16 [4096, 512], P('tok', 'head'), may hold values from -0.09375 to 0.09375
- v_weight: bfloat16 [4096, 512], P('tok', 'head'), may hold values from -0.09375 to 0.09375
- output_matrix: bfloat16 [2048, 4096], P('head', 'tok'), may hold values from -0.125 to 0.125
- key_cache: bfloat16 [64, 256, 512], P('tok', None, 'head'), may hold values from -400 to 400
- value_cache: bfloat16 [64, 256, 512], P('tok', None, 'head'), may hold values from -6 to 6
- cache_lengths: int32 [64], P('tok'), may hold values from 1 to 256
- row_request_index: int32 [8, 64], P('tok'), may hold values from 0 to 7, never falling along the last dimension, each value on 1 to 32 neighbouring positions
- ffn_gain: float32 [4096], replicated, may hold values from 0.5 to 1.5
- router_weight: bfloat16 [4096, 8], replicated, may hold values from -0.09375 to 0.09375
- routes: int32 [512, 2], P('tok'), may hold values from 0 to 7, all different within a row; in each aligned block of 64 rows (0 to 63, 64 to 127, ...) at most 18 rows name the same one
- gate_weight: bfloat16 [8, 4096, 14336], P('tok', None, 'head'), may hold values from -0.09375 to 0.09375
- up_weight: bfloat16 [8, 4096, 14336], P('tok', None, 'head'), may hold values from -0.09375 to 0.09375
- down_weight: bfloat16 [8, 14336, 4096], P('tok', None, 'head'), may hold values from -0.046875 to 0.046875
Outputs:
- layer_out: bfloat16 [512, 4096], P('tok', 'head')
Inputs may be any that keep to these rules, and one draw needn't show every extreme that they name: `row_request_index`: within the rows of one index of tok the request number never falls, every request has 1 to 32 rows, and one has exactly 32. `routes`: the two experts of a row differ; in the rows of one index of tok no expert is named more than 18 times, and that bound is reached.
All inputs are finite; a program needn't handle non-finite values.
Results may differ from a plain program's by a relative error of at most 0.012.
The roundings to bfloat16 on the way count: a program that leaves them out, or rounds other values in their place, can miss the bound.
Values may be sent and summed in bfloat16 or wider, within the bound.
A program may use at most 256 MiB of HBM per device.

v0:
```python
import jax
import jax.numpy as jnp
from jax import lax
from jax.sharding import PartitionSpec as P

D = 4096
HD = 128
Q_HEADS = 16
KV_HEADS = 4
EXPERTS = 8
CAP = 18


epsilon = 1e-05
rope_base = 1000000.0


def rms_norm(values, gain):
    values = values.astype(jnp.float32)
    factor = lax.rsqrt(jnp.mean(values * values, axis=-1, keepdims=True) + epsilon)
    return (values * factor * gain).astype(jnp.bfloat16)


def rotate(values, positions):
    half = values.shape[-1] // 2
    freqs = rope_base ** (-jnp.arange(half, dtype=jnp.float32) * 2.0 / values.shape[-1])
    angles = positions.astype(jnp.float32)[:, None] * freqs[None, :]
    cosine = jnp.concatenate([jnp.cos(angles), jnp.cos(angles)], axis=-1)[:, None, :]
    sine = jnp.concatenate([jnp.sin(angles), jnp.sin(angles)], axis=-1)[:, None, :]
    turned = jnp.concatenate([-values[..., half:], values[..., :half]], axis=-1)
    return values * cosine + turned * sine


def own_lengths(segment, lengths):
    match = segment[:, None] == jnp.arange(lengths.shape[0], dtype=jnp.int32)[None, :]
    return jnp.sum(jnp.where(match, lengths[None, :], 0), axis=1)


def row_positions(segment, lengths):
    count = segment.shape[0]
    order = jnp.arange(count, dtype=jnp.int32)
    before = jnp.sum((segment[None, :] < segment[:, None]).astype(jnp.int32), axis=1)
    return own_lengths(segment, lengths) + order - before


def attend(queries, new_keys, new_values, key_cache, value_cache, segment, lengths):
    count, kv_local, group, size = queries.shape
    requests, slots, _ = key_cache.shape
    keys = jnp.concatenate([key_cache.reshape(requests * slots, kv_local, size), new_keys], axis=0)
    values = jnp.concatenate(
        [value_cache.reshape(requests * slots, kv_local, size), new_values], axis=0
    )
    slot_index = jnp.arange(requests * slots, dtype=jnp.int32)
    slot_request = slot_index // slots
    slot_place = slot_index % slots
    limit = own_lengths(segment, lengths)
    cache_valid = (slot_request[None, :] == segment[:, None]) & (
        slot_place[None, :] < limit[:, None]
    )
    order = jnp.arange(count, dtype=jnp.int32)
    new_valid = (segment[None, :] == segment[:, None]) & (order[None, :] <= order[:, None])
    allowed = jnp.concatenate([cache_valid, new_valid], axis=1)
    scores = jnp.einsum("rhgd,khd->hgrk", queries, keys, preferred_element_type=jnp.float32)
    scores = scores / jnp.sqrt(jnp.float32(size))
    scores = jnp.where(allowed[None, None], scores, jnp.float32(-1e30))
    highest = jnp.max(scores, axis=-1, keepdims=True)
    weights = jnp.exp(scores - highest)
    probs = (weights / jnp.sum(weights, axis=-1, keepdims=True)).astype(jnp.bfloat16)
    result = jnp.einsum("hgrk,khd->rhgd", probs, values, preferred_element_type=jnp.float32)
    return result.astype(jnp.bfloat16).reshape(count, kv_local * group * size)


def slot_table(chosen):
    flat = chosen.reshape(-1)
    onehot = (flat[:, None] == jnp.arange(EXPERTS, dtype=jnp.int32)[None, :]).astype(jnp.int32)
    earlier = jnp.cumsum(onehot, axis=0) - onehot
    place = jnp.sum(earlier * onehot, axis=1)
    return flat * CAP + place


def fill_slots(normed_rows, places):
    copies = normed_rows[jnp.arange(places.shape[0], dtype=jnp.int32) // 2]
    return jnp.zeros((EXPERTS * CAP, normed_rows.shape[1]), jnp.bfloat16).at[places].set(copies)


def gate_shares(normed_rows, router_weight, chosen):
    logits = jnp.dot(normed_rows, router_weight, preferred_element_type=jnp.float32)
    match = chosen[:, :, None] == jnp.arange(EXPERTS, dtype=jnp.int32)[None, None, :]
    picked = jnp.sum(jnp.where(match, logits[:, None, :], jnp.float32(0.0)), axis=-1)
    return jax.nn.sigmoid(picked - picked[:, ::-1])


def shards(
    tokens,
    attn_gain,
    q_weight,
    k_weight,
    v_weight,
    output_matrix,
    key_cache,
    value_cache,
    cache_lengths,
    row_request_index,
    ffn_gain,
    router_weight,
    routes,
    gate_weight,
    up_weight,
    down_weight,
):
    count = tokens.shape[0]
    group = Q_HEADS // KV_HEADS
    normed = rms_norm(tokens, attn_gain)
    q_full, k_full, v_full, o_full = (
        lax.all_gather(q_weight, "tok", axis=0, tiled=True),
        lax.all_gather(k_weight, "tok", axis=0, tiled=True),
        lax.all_gather(v_weight, "tok", axis=0, tiled=True),
        lax.all_gather(output_matrix, "tok", axis=1, tiled=True),
    )
    kv_local = k_full.shape[1] // HD
    queries = jnp.dot(normed, q_full, preferred_element_type=jnp.float32)
    keys_new = jnp.dot(normed, k_full, preferred_element_type=jnp.float32)
    values_new = jnp.dot(normed, v_full, preferred_element_type=jnp.float32)
    segment = row_request_index[0]
    positions = row_positions(segment, cache_lengths)
    queries = rotate(queries.reshape(count, kv_local * group, HD), positions).astype(jnp.bfloat16)
    queries = queries.reshape(count, kv_local, group, HD)
    keys_new = rotate(keys_new.reshape(count, kv_local, HD), positions).astype(jnp.bfloat16)
    values_new = values_new.astype(jnp.bfloat16).reshape(count, kv_local, HD)
    attn = attend(queries, keys_new, values_new, key_cache, value_cache, segment, cache_lengths)
    partial_mix = jnp.dot(attn, o_full, preferred_element_type=jnp.float32)
    mixed = lax.psum(partial_mix, "head")
    hidden_activation = tokens.astype(jnp.float32) + mixed
    normed_ffn = rms_norm(hidden_activation, ffn_gain)
    shares = gate_shares(normed_ffn, router_weight, routes)
    places = slot_table(routes)
    buffer = fill_slots(normed_ffn, places)
    owners = lax.axis_size("tok")
    slices = owners // EXPERTS
    quarter = down_weight.shape[2]
    head_index = lax.axis_index("head")
    outgoing = jnp.broadcast_to(
        buffer.reshape(EXPERTS, 1, CAP, D), (EXPERTS, slices, CAP, D)
    ).reshape(owners, CAP, D)
    arrived = lax.all_to_all(outgoing, "tok", split_axis=0, concat_axis=0, tiled=True)
    active = jnp.einsum("tcd,df->tcf", arrived, gate_weight[0], preferred_element_type=jnp.float32)
    linear = jnp.einsum("tcd,df->tcf", arrived, up_weight[0], preferred_element_type=jnp.float32)
    hidden = (jax.nn.silu(active) * linear).astype(jnp.bfloat16)
    hidden_all = lax.all_gather(hidden, "head", axis=2, tiled=True)
    output = jnp.einsum(
        "tcf,fd->tcd", hidden_all, down_weight[0], preferred_element_type=jnp.float32
    )
    layer_results = output.astype(jnp.bfloat16)
    returned = lax.all_to_all(layer_results, "tok", split_axis=0, concat_axis=0, tiled=True)
    summed = jnp.sum(returned.reshape(EXPERTS, slices, CAP, quarter).astype(jnp.float32), axis=1)
    summed = summed.reshape(EXPERTS * CAP, quarter)
    picked = jnp.take(summed, places, axis=0).reshape(count, 2, quarter)
    mixture = jnp.sum(shares[:, :, None] * picked, axis=1)
    residual = lax.dynamic_slice_in_dim(hidden_activation, head_index * quarter, quarter, 1)
    return (residual + mixture).astype(jnp.bfloat16)


def solution(mesh):
    in_specs = (
        P("tok", None),
        P(),
        P("tok", "head"),
        P("tok", "head"),
        P("tok", "head"),
        P("head", "tok"),
        P("tok", None, "head"),
        P("tok", None, "head"),
        P("tok"),
        P("tok", None),
        P(),
        P(),
        P("tok", None),
        P("tok", None, "head"),
        P("tok", None, "head"),
        P("tok", None, "head"),
    )
    out_specs = P("tok", "head")
    return jax.shard_map(shards, mesh=mesh, in_specs=in_specs, out_specs=out_specs, check_vma=False)
```

profile of v0, /device:TPU:0, one launch (start us, length us, event | category | flops | bytes accessed | tf_op | source)
XLA Modules:
  0.0 441.3 jit_solution(15756063312826419682)
XLA Ops:
  11.5 0.9 convert_reduce_fusion
  13.2 1.2 fusion.21
  14.4 0.8 fusion.42
  15.7 36.7 %all-gather.6.cloned.1.call-done = bf16[4096,128]{1,0:T(8,128)(2,1)} async-done(((bf16[512,128]{1,0:T(8,128)(2,1)}), bf16[4096,128]{1,0:T(8,128)(2,1)}) %all-gather.6.cloned.1.call-update) | async-done | bytes 1048592 | tf_op jit(solution)/shard_map/all_gather | solution.py:117
  52.4 1.6 fusion.20
  54.0 39.5 %all-gather.8.cloned.1.call-done = bf16[4096,128]{1,0:T(8,128)(2,1)} async-done(((bf16[512,128]{1,0:T(8,128)(2,1)}), bf16[4096,128]{1,0:T(8,128)(2,1)}) %all-gather.8.cloned.1.call-update) | async-done | bytes 1048592 | tf_op jit(solution)/shard_map/all_gather | solution.py:116
  93.4 1.6 fusion.57
  95.2 72.5 %all-gather.10.cloned.1.call-done = bf16[4096,512]{1,0:T(8,128)(2,1)} async-done(((bf16[512,512]{1,0:T(8,128)(2,1)}), bf16[4096,512]{1,0:T(8,128)(2,1)}) %all-gather.10.cloned.1.call-update) | async-done | bytes 4194320 | tf_op jit(solution)/shard_map/all_gather | solution.py:115
  167.8 3.1 fusion.55
  172.9 70.0 %all-gather.12.cloned.1.call-done = bf16[512,4096]{1,0:T(8,128)(2,1)} async-done(((bf16[512,512]{1,0:T(8,128)(2,1)}), bf16[512,4096]{1,0:T(8,128)(2,1)}) %all-gather.12.cloned.1.call-update) | async-done | bytes 4194320 | tf_op jit(solution)/shard_map/all_gather | solution.py:118
  243.0 4.0 fusion.33
  247.3 34.1 %all-reduce.2.cloned.1.call-done = f32[64,4096]{1,0:T(8,128)} async-done(((f32[64,4096]{1,0:T(8,128)}), f32[64,4096]{1,0:T(8,128)}) %all-reduce.2.cloned.1.call-update) | async-done | bytes 1048592 | tf_op jit(solution)/shard_map/psum | solution.py:132
  281.4 1.5 multiply_reduce_fusion
  283.1 6.2 %scatter_custom_fusion = bf16[144,4096]{1,0:T(8,128)(2,1)} fusion(s32[128]{0:T(128)S(1)} %fusion.52, bf16[64,4096]{1,0:T(8,128)(2,1)S(1)} %multiply_convert_fusion, s32[1024]{0:T(1024)S(1)} %pad_clamp_fusion.1, bf16[]{:T(256)} %constant.104.clone.1), kind=kCustom, calls=%fused_computation.29 | custom fusion | bytes 1179650 | tf_op jit(solution)/shard_map/scatter | solution.py:83
  289.2 1.4 reshape_reshape.3
  290.7 41.9 %all_to_all.10 = bf16[8,18,4096]{2,1,0:T(8,128)(2,1)S(1)} all-to-all(bf16[8,18,4096]{2,1,0:T(8,128)(2,1)S(1)} %reshape_reshape.3), channel_id=1, replica_groups=mesh['head'=4,'tok'=8] {'tok'}, dimensions={0} | all-to-all | bytes 2359296 | tf_op jit(solution)/shard_map/all_to_all | solution.py:145
  332.6 12.5 %fusion.4 = f32[8,18,3584]{2,1,0:T(8,128)S(1)} fusion(bf16[8,18,4096]{2,1,0:T(8,128)(2,1)S(1)} %all_to_all.10, bf16[1,4096,3584]{2,1,0:T(8,128)(2,1)} %param.29), kind=kOutput, calls=%fused_computation.7 | convolution fusion | flops 4227858432 | bytes 32604160 | tf_op jit(solution)/shard_map/tcd,df->tcf/dot_general | solution.py:146
  345.1 13.5 %fusion.9 = bf16[8,18,3584]{2,1,0:T(8,128)(2,1)} fusion(bf16[8,18,4096]{2,1,0:T(8,128)(2,1)S(1)} %all_to_all.10, bf16[1,4096,3584]{2,1,0:T(8,128)(2,1)} %param.30, f32[8,18,3584]{2,1,0:T(8,128)S(1)} %fusion.4), kind=kOutput, calls=%fused_computation.10 | convolution fusion | flops 4230955008 | bytes 33636352 | tf_op jit(solution)/shard_map/tcd,df->tcf/dot_general | solution.py:147
  359.0 40.4 %all-gather.14.cloned.1.call-done = bf16[8,18,14336]{2,1,0:T(8,128)(2,1)} async-done(((bf16[8,18,3584]{2,1,0:T(8,128)(2,1)}), bf16[8,18,14336]{2,1,0:T(8,128)(2,1)}) %all-gather.14.cloned.1.call-update) | async-done | bytes 4128784 | tf_op jit(solution)/shard_map/all_gather | solution.py:149
  399.4 14.7 %fusion.15 = bf16[8,18,1024]{2,1,0:T(8,128)(2,1)} fusion(bf16[8,18,14336]{2,1,0:T(8,128)(2,1)} %all-gather.14.cloned.1.call-done, bf16[1,14336,1024]{2,1,0:T(8,128)(2,1)} %param.31), kind=kOutput, calls=%fused_computation.20 | convolution fusion | flops 4228005888 | bytes 33783808 | tf_op jit(solution)/shard_map/tcf,fd->tcd/dot_general | solution.py:150
  414.1 5.5 %all-to-all-start.1 = ((bf16[8,18,1024]{2,1,0:T(8,128)(2,1)}), bf16[8,18,1024]{2,1,0:T(8,128)(2,1)S(1)}, u32[]{:S(2)}, u32[]{:S(2)}) async-start(bf16[8,18,1024]{2,1,0:T(8,128)(2,1)} %fusion.15), calls=%async_computation.1 | async-start | bytes 786432 | tf_op jit(solution)/shard_map/all_to_all | solution.py:154
  420.0 11.7 %all-to-all-done.1 = bf16[8,18,1024]{2,1,0:T(8,128)(2,1)S(1)} async-done(((bf16[8,18,1024]{2,1,0:T(8,128)(2,1)}), bf16[8,18,1024]{2,1,0:T(8,128)(2,1)S(1)}, u32[]{:S(2)}, u32[]{:S(2)}) %all-to-all-start.1) | async-done | bytes 294944 | tf_op jit(solution)/shard_map/all_to_all | solution.py:154
  431.8 0.8 gather_fusion
  432.9 0.8 multiply_reduce_fusion.1
  (72 shorter events, 10.5 us)
Async XLA Ops:
  6.5 413.1 %copy-start = (bf16[4096,8]{0,1:T(8,128)(2,1)S(1)}, bf16[4096,8]{0,1:T(8,128)(2,1)}, u32[]{:S(2)}) copy-start(bf16[4096,8]{0,1:T(8,128)(2,1)} %param.27) | copy-start | bytes 196612
  6.5 8.9 %copy-start.5 = (s32[1,64]{1,0:T(1,128)S(1)}, s32[1,64]{1,0:T(1,128)}, u32[]{:S(2)}) copy-start(s32[1,64]{1,0:T(1,128)} %param.25) | copy-start | bytes 772
  6.5 45.8 %copy-start.1 = (bf16[64,4096]{1,0:T(8,128)(2,1)S(1)}, bf16[64,4096]{1,0:T(8,128)(2,1)}, u32[]{:S(2)}) copy-start(bf16[64,4096]{1,0:T(8,128)(2,1)} %param.16) | copy-start | bytes 1572868
  6.5 45.8 %copy-start.2 = (f32[4096]{0:T(1024)S(1)}, f32[4096]{0:T(1024)}, u32[]{:S(2)}) copy-start(f32[4096]{0:T(1024)} %param.17) | copy-start | bytes 49156
  6.5 45.8 %all-gather.6.cloned.1.call-start = ((), (), s32[]{:S(2)}) async-start(), calls=%async_computation.2 | async-start | bytes 1179648 | tf_op jit(solution)/shard_map/all_gather | solution.py:117
  7.3 86.2 %all-gather.8.cloned.1.call-start = ((), (), s32[]{:S(2)}) async-start(), calls=%async_computation.3 | async-start | bytes 1179648 | tf_op jit(solution)/shard_map/all_gather | solution.py:116
  8.0 159.7 %all-gather.10.cloned.1.call-start = ((), (), s32[]{:S(2)}) async-start(), calls=%async_computation.4 | async-start | bytes 4718592 | tf_op jit(solution)/shard_map/all_gather | solution.py:115
  8.8 234.2 %all-gather.12.cloned.1.call-start = ((), (), s32[]{:S(2)}) async-start(), calls=%async_computation.5 | async-start | bytes 4718592 | tf_op jit(solution)/shard_map/all_gather | solution.py:118
  9.3 272.1 %all-reduce.2.cloned.1.call-start = ((), (), s32[]{:S(2)}) async-start(), calls=%async_computation.6 | async-start | bytes 2097152 | tf_op jit(solution)/shard_map/psum | solution.py:132
  95.2 76.0 %copy-start.6 = (bf16[8,256,128]{2,1,0:T(8,128)(2,1)S(1)}, bf16[8,256,128]{2,1,0:T(8,128)(2,1)}, u32[]{:S(2)}) copy-start(bf16[8,256,128]{2,1,0:T(8,128)(2,1)} %param.22) | copy-start | bytes 1572868
  171.2 1.1 copy-start.7
  247.0 35.9 %copy-start.3 = (f32[4096]{0:T(1024)S(1)}, f32[4096]{0:T(1024)}, u32[]{:S(2)}) copy-start(f32[4096]{0:T(1024)} %param.26) | copy-start | bytes 49156
  247.0 152.4 %all-gather.14.cloned.1.call-start = ((), (), s32[]{:S(2)}) async-start(), calls=%async_computation.7 | async-start | bytes 6881280 | tf_op jit(solution)/shard_map/all_gather | solution.py:149
  345.1 13.7 %copy-start.4 = (s32[64,2]{0,1:T(2,128)S(1)}, s32[64,2]{0,1:T(2,128)}, u32[]{:S(2)}) copy-start(s32[64,2]{0,1:T(2,128)} %param.28) | copy-start | bytes 1540
  414.1 17.6 %all-to-all-start.1 = ((bf16[8,18,1024]{2,1,0:T(8,128)(2,1)}), bf16[8,18,1024]{2,1,0:T(8,128)(2,1)S(1)}, u32[]{:S(2)}, u32[]{:S(2)}) async-start(bf16[8,18,1024]{2,1,0:T(8,128)(2,1)} %fusion.15), calls=%async_computation.1 | async-start | bytes 786432 | tf_op jit(solution)/shard_map/all_to_all | solution.py:154
Sparse Core Ops, SparseCore 0:
  9.5 42.8 all-gather.5
  54.5 38.8 all-gather.7
  95.6 72.1 all-gather.9
  169.7 73.2 all-gather.11
  247.1 34.2 all-reduce.1
  358.7 40.6 all-gather.13
where the time goes:
time: 442 us; the launch traced here: 441 us
  waiting for transfers between devices  308 us (70%)
  matrix products  52.4 us (12%)
  blocking collectives  41.9 us (9%)
  between operations  13.8 us (3%)
  local copies, waits for them, and re-layouts  10.5 us (2%)
  other arithmetic  9.38 us (2%)
  starting transfers between devices  5.74 us (1%)
    all_gather x1, waiting for transfers between devices, shards(): lax.all_gather(q_weight, 'tok', axis=0, tiled=True)  72.5 us
    all_gather x1, waiting for transfers between devices, shards(): lax.all_gather(output_matrix, 'tok', axis=1, tiled=True)  70 us
    all_to_all x1, blocking collectives, shards(): lax.all_to_all(outgoing, 'tok', split_axis=0, concat_axis=0, tiled=True)  41.9 us
    all_gather x1, waiting for transfers between devices, shards(): hidden_all = lax.all_gather(hidden, 'head', axis=2, tiled=True)  40.4 us
    all_gather x1, waiting for transfers between devices, shards(): lax.all_gather(k_weight, 'tok', axis=0, tiled=True)  39.5 us
    all_gather x1, waiting for transfers between devices, shards(): lax.all_gather(v_weight, 'tok', axis=0, tiled=True)  36.7 us
    psum x1, waiting for transfers between devices, shards(): mixed = lax.psum(partial_mix, 'head')  34.1 us
    dot_general x1, matrix products, shards(): jnp.einsum('tcf,fd->tcd', hidden_all, down_weight[0], preferred_element_t...  14.7 us
  transfers between devices with their start and end apart: 7, of which 7 were waited for; matrix products, arithmetic and copies ran while one was open for 4% of the time, Pallas kernels for 0%

commit v1 on v0

--- a/solution.py
+++ b/solution.py
@@ -1,6 +1,11 @@
+import functools
+
 import jax
 import jax.numpy as jnp
+import numpy as np
 from jax import lax
+from jax.experimental import pallas as pl
+from jax.experimental.pallas import tpu as pltpu
 from jax.sharding import PartitionSpec as P
 
 D = 4096
@@ -160,6 +165,515 @@
     return (residual + mixture).astype(jnp.bfloat16)
 
 
+MESH = pl.DeviceIdType.MESH
+F32 = jnp.float32
+BF16 = jnp.bfloat16
+MAIN = 16
+NW = 3
+ND = 12
+FC = 512
+
+
+def rcopy(src, dst, send_sem, recv_sem, head, tok):
+    return pltpu.make_async_remote_copy(
+        src_ref=src, dst_ref=dst, send_sem=send_sem, recv_sem=recv_sem,
+        device_id={"head": head, "tok": tok}, device_id_type=MESH,
+    )
+
+
+def mm(a, b):
+    return jnp.dot(a, b, preferred_element_type=F32)
+
+
+def relatives(head):
+    core, side = lax.rem(head, 2), head // 2
+    return head, side * 2 + 1 - core, (1 - side) * 2 + core, (1 - side) * 2 + 1 - core
+
+
+def ahead(me, n, s):
+    return lax.rem(me // 2 + s // 2, n // 2) * 2 + (lax.rem(me + s % 2, 2))
+
+
+def behind(me, n, s):
+    return lax.rem(me // 2 + n // 2 - s // 2, n // 2) * 2 + (lax.rem(me + s % 2, 2))
+
+
+def project_kernel(n, m, tok_ref, gain_ref, q_ref, k_ref, v_ref, out_ref,
+                   nrm, xin, keep, parta, pa, partb, pb, s1, r1, s3, r3, s2, r2, s4, r4):
+    me = lax.axis_index("tok")
+    head = lax.axis_index("head")
+    heads = relatives(head)
+    barrier = pltpu.get_barrier_semaphore()
+    for d in range(1, n):
+        pl.semaphore_signal(barrier, inc=1, device_id={"head": head, "tok": lax.rem(me + d, n)},
+                            device_id_type=MESH)
+    for i in range(1, m):
+        pl.semaphore_signal(barrier, inc=1, device_id={"head": heads[i], "tok": me},
+                            device_id_type=MESH)
+    values = tok_ref[...].astype(F32)
+    factor = lax.rsqrt(jnp.mean(values * values, axis=-1, keepdims=True) + epsilon)
+    normed = (values * factor * gain_ref[...]).astype(BF16)
+    width = normed.shape[1] // n
+    for j in range(n):
+        nrm[j] = normed[:, j * width:(j + 1) * width]
+    pl.semaphore_wait(barrier, n + m - 2)
+    share_rows = normed.shape[0] // m
+
+    def rows(h):
+        return pl.ds(pl.multiple_of(h * share_rows, share_rows), share_rows)
+
+    def first(s):
+        to = ahead(me, n, s)
+        return rcopy(nrm.at[to, rows(head)], xin.at[s, rows(head)], s1.at[s], r1.at[s], head, to)
+
+    def share(s, i):
+        part = xin.at[s, rows(head)]
+        return rcopy(part, part, s3.at[s, i], r3.at[s, i], heads[i], me)
+
+    def shared(s, i):
+        part = xin.at[s, rows(heads[i])]
+        return rcopy(part, part, s3.at[s, i], r3.at[s, i], heads[i], me)
+
+    def across(z):
+        return rcopy(parta.at[z], pa.at[z], s2.at[z], r2.at[z], head, ahead(me, n, 1))
+
+    def along(z):
+        return rcopy(partb.at[z], pb.at[z], s4.at[z], r4.at[z], head, behind(me, n, 2 * z))
+
+    def project(x):
+        return jnp.concatenate([mm(x, q_ref[...]), mm(x, k_ref[...]), mm(x, v_ref[...])], axis=1)
+
+    order = [3, 2, 5, 4, 7, 6, 1]
+    for s in order:
+        first(s).start()
+    keep[0] = project(nrm[me])
+    for s in order:
+        first(s).wait_recv()
+        for i in (2, 3, 1):
+            share(s, i).start()
+
+    def pass_on(z):
+        across(z).wait_recv()
+        if z == 0:
+            keep[0] += pa[0].astype(F32)
+        else:
+            partb[z] = (keep[z] + pa[z].astype(F32)).astype(BF16)
+            along(z).start()
+
+    for s in order:
+        for i in range(1, m):
+            shared(s, i).wait_recv()
+        z = s // 2
+        if s % 2:
+            parta[z] = project(xin[s]).astype(BF16)
+            across(z).start()
+            if z == 0:
+                pass_on(n // 2 - 1)
+                pass_on(0)
+        else:
+            keep[z] = project(xin[s])
+            if z > 1:
+                pass_on(z - 1)
+    total = keep[0]
+    for z in range(1, n // 2):
+        along(z).wait_recv()
+        total = total + pb[z].astype(F32)
+    out_ref[...] = total
+    for s in order:
+        first(s).wait_send()
+        for i in range(1, m):
+            share(s, i).wait_send()
+    for z in range(n // 2):
+        across(z).wait_send()
+        if z > 0:
+            along(z).wait_send()
+
+
+def project(n, m, tokens, gain, q_weight, k_weight, v_weight):
+    rows, width = tokens.shape
+    cols = q_weight.shape[1] + k_weight.shape[1] + v_weight.shape[1]
+    dma = pltpu.SemaphoreType.DMA
+    return pl.pallas_call(
+        functools.partial(project_kernel, n, m),
+        out_shape=jax.ShapeDtypeStruct((rows, cols), F32),
+        in_specs=[pl.BlockSpec(memory_space=pltpu.VMEM)] * 5,
+        out_specs=pl.BlockSpec(memory_space=pltpu.VMEM),
+        scratch_shapes=[
+            pltpu.VMEM((n, rows, width // n), BF16),
+            pltpu.VMEM((n, rows, width // n), BF16),
+            pltpu.VMEM((n // 2, rows, cols), F32),
+            pltpu.VMEM((n // 2, rows, cols), BF16),
+            pltpu.VMEM((n // 2, rows, cols), BF16),
+            pltpu.VMEM((n // 2, rows, cols), BF16),
+            pltpu.VMEM((n // 2, rows, cols), BF16),
+            dma((n,)), dma((n,)), dma((n, m)), dma((n, m)),
+            dma((n // 2,)), dma((n // 2,)), dma((n // 2,)), dma((n // 2,)),
+        ],
+        compiler_params=pltpu.CompilerParams(collective_id=0, has_side_effects=True),
+    )(tokens, gain.reshape(1, -1), q_weight, k_weight, v_weight)
+
+
+def experts_kernel(n, m, attn_ref, w_ref, tok_ref, gain_ref, router_ref, pmain_ref, ptail_ref,
+                   sel_ref, seltail_ref, fold_ref, unfold_ref, chosen_ref, gate_ref, up_ref, down_ref,
+                   out_ref,
+                   ain, part, pin, stat, logit, xs, xin, xall, gbuf, ubuf, hall, dbuf, acc, yout, yin,
+                   hid_ref,
+                   sa, ra, sp, rp, ss, rs, sl, rl, sx, rx, sg, rg, sh, rh, sy, ry, gsem, usem, dsem):
+    me = lax.axis_index("tok")
+    head = lax.axis_index("head")
+    heads = relatives(head)
+    sib = heads[1]
+    steps = gate_ref.shape[2] // FC
+    local = gate_ref.shape[2]
+    quarter = tok_ref.shape[1]
+    total = n * m
+    flat = head * n + me
+    barrier = pltpu.get_barrier_semaphore()
+
+    @pl.loop(1, total)
+    def _(d):
+        other = lax.rem(flat + d, total)
+        pl.semaphore_signal(barrier, inc=1, device_id={"head": other // n, "tok": lax.rem(other, n)},
+                            device_id_type=MESH)
+
+    def wcopies(j, slot):
+        cols = pl.ds(pl.multiple_of(j * FC, FC), FC)
+        return (pltpu.make_async_copy(gate_ref.at[0, :, cols], gbuf.at[slot], gsem.at[slot]),
+                pltpu.make_async_copy(up_ref.at[0, :, cols], ubuf.at[slot], usem.at[slot]))
+
+    def dcopy(r, j, slot):
+        which = heads[0]
+        for i in range(1, m):
+            which = jnp.where(r == i, heads[i], which)
+        start = pl.multiple_of(which * local + j * FC, FC)
+        return pltpu.make_async_copy(down_ref.at[0, pl.ds(start, FC), :], dbuf.at[slot], dsem.at[slot])
+
+    for j in range(NW):
+        for c in wcopies(j, j):
+            c.start()
+    for k in range(ND):
+        dcopy(k // steps, k % steps, k).start()
+    pl.semaphore_wait(barrier, total - 1)
+
+    group = n // m
+    target = me // group
+    myslot = head * group + lax.rem(me, group)
+
+    def acopy(s):
+        if s > 1 and s % 2:
+            return rcopy(ain.at[s - 1], ain.at[s], sa.at[s], ra.at[s], head, ahead(me, n, 1))
+        return rcopy(attn_ref, ain.at[s], sa.at[s], ra.at[s], head, ahead(me, n, s))
+
+    def pcopy(s):
+        return rcopy(part.at[s], pin.at[myslot], sp.at[s], rp.at[myslot], target, behind(me, n, s))
+
+    for s in [*range(2, n, 2), 1]:
+        acopy(s).start()
+    own = mm(attn_ref[...], w_ref[...]).astype(BF16)
+    mine = head == target
+
+    @pl.when(mine)
+    def _():
+        pin[myslot] = own
+
+    @pl.when(jnp.logical_not(mine))
+    def _():
+        part[0] = own
+        pcopy(0).start()
+
+    def mixed(s):
+        part[s] = mm(ain[s], w_ref[...]).astype(BF16)
+        pcopy(s).start()
+
+    acopy(1).wait_recv()
+    mixed(1)
+    for s in range(2, n, 2):
+        acopy(s).wait_recv()
+        acopy(s + 1).start()
+        mixed(s)
+        if s > 2:
+            acopy(s - 1).wait_recv()
+            mixed(s - 1)
+    acopy(n - 1).wait_recv()
+    mixed(n - 1)
+    for s in range(m * group):
+        @pl.when(jnp.logical_not(mine & (myslot == s)))
+        def _():
+            rcopy(part.at[0], pin.at[s], sp.at[0], rp.at[s], sib, me).wait_recv()
+    hidden = tok_ref[...].astype(F32)
+    sums = []
+    for g in range(group):
+        t = pin[g].astype(F32)
+        for h in range(1, m):
+            t = t + pin[h * group + g].astype(F32)
+        sums.append(t)
+    hidden = hidden + jnp.concatenate(sums, axis=1)
+    hid_ref[...] = hidden
+
+    def exchange(buf, ssem, rsem, i):
+        return rcopy(buf.at[0], buf.at[i], ssem.at[i], rsem.at[i], heads[i], me)
+
+    stat[0] = jnp.broadcast_to(jnp.sum(hidden * hidden, axis=-1, keepdims=True), stat.shape[1:])
+    for i in range(1, m):
+        exchange(stat, ss, rs, i).start()
+    for i in range(1, m):
+        exchange(stat, ss, rs, i).wait_recv()
+    square = stat[0]
+    for i in range(1, m):
+        square = square + stat[i]
+    factor = lax.rsqrt(square[:, :1] / (quarter * m) + epsilon)
+    normed = (hidden * factor * gain_ref[...]).astype(BF16)
+
+    main = mm(pmain_ref[...], normed).astype(BF16)
+    chunks = quarter // 128
+    tail = mm(ptail_ref[0], normed[:, :128])
+    for c in range(1, chunks):
+        tail = tail + mm(ptail_ref[c], normed[:, c * 128:(c + 1) * 128])
+    tail = tail.astype(BF16)
+    for e in range(n):
+        xs[e, :, :quarter] = main[e * MAIN:(e + 1) * MAIN]
+        xs[e, :, quarter:] = tail[e * MAIN:(e + 1) * MAIN]
+
+    def xcopy(d):
+        to = lax.rem(me + d, n)
+        return rcopy(xs.at[to], xin.at[d], sx.at[d], rx.at[d], head, to)
+
+    for d in range(1, n):
+        xcopy(d).start()
+    xin[0] = xs[me]
+    logit[0] = mm(normed, router_ref[...])
+    for i in range(1, m):
+        exchange(logit, sl, rl, i).start()
+    for d in range(1, n):
+        xcopy(d).wait_recv()
+    for d in range(n):
+        xall[0, d * MAIN:(d + 1) * MAIN] = xin[d, :, :quarter]
+    tails = jnp.concatenate([xin[d, :, quarter:] for d in range(n)], axis=0)
+    for c in range(chunks):
+        xall[0, n * MAIN:, c * 128:(c + 1) * 128] = mm(fold_ref[c], tails).astype(BF16)
+
+    def gcopy(i):
+        if i == 3:
+            return rcopy(xall.at[2], xall.at[3], sg.at[3], rg.at[3], sib, me)
+        return rcopy(xall.at[0], xall.at[i], sg.at[i], rg.at[i], heads[i], me)
+
+    gcopy(2).start()
+    gcopy(1).start()
+    gcopy(2).wait_recv()
+    gcopy(3).start()
+    gcopy(1).wait_recv()
+    gcopy(3).wait_recv()
+
+    def hcopy(i, j):
+        if i == 3:
+            return rcopy(hall.at[2, j], hall.at[3, j], sh.at[3, j], rh.at[3, j], sib, me)
+        return rcopy(hall.at[0, j], hall.at[i, j], sh.at[i, j], rh.at[i, j], heads[i], me)
+
+    lag = 2
+
+    def forward(j):
+        hcopy(2, j).wait_recv()
+        hcopy(3, j).start()
+
+    @pl.loop(0, steps)
+    def _(j):
+        slot = lax.rem(j, NW)
+        for c in wcopies(j, slot):
+            c.wait()
+        g = jnp.zeros((xall.shape[1], FC), F32)
+        u = jnp.zeros((xall.shape[1], FC), F32)
+        for i in range(m):
+            rows = pl.ds(pl.multiple_of(heads[i] * quarter, quarter), quarter)
+            g = g + mm(xall[i], gbuf[slot, rows, :])
+            u = u + mm(xall[i], ubuf[slot, rows, :])
+        hall[0, j] = ((g / (1.0 + jnp.exp(-g))) * u).astype(BF16)
+        hcopy(2, j).start()
+        hcopy(1, j).start()
+
+        @pl.when(j + NW < steps)
+        def _():
+            for c in wcopies(j + NW, slot):
+                c.start()
+
+        @pl.when(j >= lag)
+        def _():
+            forward(j - lag)
+
+    acc[...] = jnp.zeros_like(acc)
+
+    def segment(r):
+        @pl.loop(0, steps)
+        def _(j):
+            k = r * steps + j
+            slot = lax.rem(k, ND)
+            if r in (1, 3):
+                hcopy(r, j).wait_recv()
+            dcopy(r, j, slot).wait()
+            acc[...] += mm(hall[r, j], dbuf[slot])
+
+            @pl.when(k + ND < m * steps)
+            def _():
+                dcopy((k + ND) // steps, lax.rem(k + ND, steps), slot).start()
+
+    segment(0)
+    forward(steps - 2)
+    segment(1)
+    forward(steps - 1)
+    segment(2)
+    segment(3)
+
+    result = acc[...].astype(BF16)
+    rest = result[n * MAIN:]
+    back = mm(unfold_ref[0], rest[:, :128])
+    for c in range(1, chunks):
+        back = back + mm(unfold_ref[c], rest[:, c * 128:(c + 1) * 128])
+    back = back.astype(BF16)
+
+    def ycopy(d):
+        return rcopy(yout.at[d], yin.at[me], sy.at[d], ry.at[d], head, lax.rem(me + n - d, n))
+
+    for d in range(n):
+        yout[d, :, :quarter] = result[d * MAIN:(d + 1) * MAIN]
+        yout[d, :, quarter:] = back[d * MAIN:(d + 1) * MAIN]
+        if d > 0:
+            ycopy(d).start()
+    yin[me] = yout[0]
+
+    for i in range(1, m):
+        exchange(logit, sl, rl, i).wait_recv()
+    logits = logit[0]
+    for i in range(1, m):
+        logits = logits + logit[i]
+    lane = lax.broadcasted_iota(jnp.int32, logits.shape, 1)
+    picks = [jnp.sum(jnp.where(lane == chosen_ref[:, k:k + 1], logits, 0.0), axis=-1, keepdims=True)
+             for k in range(2)]
+    shares = [jax.nn.sigmoid(picks[0] - picks[1]), jax.nn.sigmoid(picks[1] - picks[0])]
+
+    for d in range(1, n):
+        rcopy(yout.at[d], yin.at[lax.rem(me + d, n)], sy.at[d], ry.at[d], head, me).wait_recv()
+    mains = jnp.concatenate([yin[e, :, :quarter] for e in range(n)], axis=0)
+    ends = jnp.concatenate([yin[e, :, quarter:] for e in range(n)], axis=0)
+    mixture = None
+    for k in range(2):
+        wide = jnp.concatenate([mm(seltail_ref[k * chunks + c], ends) for c in range(chunks)], axis=1)
+        term = shares[k] * (mm(sel_ref[k], mains) + wide)
+        mixture = term if mixture is None else mixture + term
+    out_ref[...] = (hid_ref[...] + mixture).astype(BF16)
+
+    for d in range(1, n):
+        acopy(d).wait_send()
+        pcopy(d).wait_send()
+        xcopy(d).wait_send()
+        ycopy(d).wait_send()
+
+    @pl.when(jnp.logical_not(mine))
+    def _():
+        pcopy(0).wait_send()
+
+    for i in range(1, m):
+        exchange(stat, ss, rs, i).wait_send()
+        exchange(logit, sl, rl, i).wait_send()
+        gcopy(i).wait_send()
+
+        @pl.loop(0, steps)
+        def _(j):
+            hcopy(i, j).wait_send()
+
+
+def experts(n, m, attn, weight, tokens, gain, router, tables, chosen, gate, up, down):
+    rows, quarter = tokens.shape
+    deep, wide = weight.shape
+    slots = n * CAP
+    steps = gate.shape[2] // FC
+    dma = pltpu.SemaphoreType.DMA
+    vm = pl.BlockSpec(memory_space=pltpu.VMEM)
+    hbm = pl.BlockSpec(memory_space=pltpu.HBM)
+    return pl.pallas_call(
+        functools.partial(experts_kernel, n, m),
+        out_shape=jax.ShapeDtypeStruct((rows, quarter), BF16),
+        in_specs=[vm] * 12 + [hbm] * 3,
+        out_specs=vm,
+        scratch_shapes=[
+            pltpu.VMEM((n, rows, deep), BF16),
+            pltpu.VMEM((n, rows, wide), BF16),
+            pltpu.VMEM((n, rows, wide), BF16),
+            pltpu.VMEM((m, rows, 128), F32),
+            pltpu.VMEM((m, rows, 128), F32),
+            pltpu.VMEM((n, MAIN, quarter + 128), BF16),
+            pltpu.VMEM((n, MAIN, quarter + 128), BF16),
+            pltpu.VMEM((m, slots, quarter), BF16),
+            pltpu.VMEM((NW, gate.shape[1], FC), BF16),
+            pltpu.VMEM((NW, gate.shape[1], FC), BF16),
+            pltpu.VMEM((m, steps, slots, FC), BF16),
+            pltpu.VMEM((ND, FC, quarter), BF16),
+            pltpu.VMEM((slots, quarter), F32),
+            pltpu.VMEM((n, MAIN, quarter + 128), BF16),
+            pltpu.VMEM((n, MAIN, quarter + 128), BF16),
+            pltpu.VMEM((rows, quarter), F32),
+            dma((n,)), dma((n,)), dma((n,)), dma((n,)),
+            dma((m,)), dma((m,)), dma((m,)), dma((m,)),
+            dma((n,)), dma((n,)), dma((m,)), dma((m,)),
+            dma((m, steps)), dma((m, steps)), dma((n,)), dma((n,)),
+            dma((NW,)), dma((NW,)), dma((ND,)),
+        ],
+        compiler_params=pltpu.CompilerParams(
+            collective_id=1, has_side_effects=True, vmem_limit_bytes=60 * 1024 * 1024),
+    )(attn, weight, tokens, gain, router, *tables, chosen, gate, up, down)
+
+
+def slot_tables(chosen, chunks):
+    places = slot_table(chosen).reshape(chosen.shape)
+    slot = places - chosen * CAP
+    more = CAP - MAIN
+    where = jnp.arange(EXPERTS * MAIN, dtype=jnp.int32)
+    expert, place = where // MAIN, where % MAIN
+    match = chosen[:, :, None] == expert
+    sel = match & (slot[:, :, None] == place)
+    chunk = jnp.arange(chunks, dtype=jnp.int32)[:, None]
+    end = (place // more == chunk) & (place % more >= 0)
+    seltail = (match & (slot[:, :, None] == MAIN + place % more))[:, :, None, :] & end
+    sel = sel.transpose(1, 0, 2)
+    seltail = seltail.transpose(1, 2, 0, 3)
+    pmain = (sel[0] | sel[1]).T
+    ptail = (seltail[0] | seltail[1]).transpose(0, 2, 1)
+    group = np.arange(EXPERTS * more)
+    spot = np.arange(EXPERTS * MAIN)
+    fold = (group[:, None] // more == spot // MAIN) & (group[:, None] % more == spot % more)
+    fold = fold[None] & (spot % MAIN // more == np.arange(chunks)[:, None])[:, None, :]
+    unfold = fold.transpose(0, 2, 1)
+    seltail = seltail.reshape(2 * chunks, chosen.shape[0], -1)
+    return [jnp.asarray(a, BF16) for a in (pmain, ptail, sel, seltail, fold, unfold)]
+
+
+def shards_eight(
+    tokens, attn_gain, q_weight, k_weight, v_weight, output_matrix, key_cache, value_cache,
+    cache_lengths, row_request_index, ffn_gain, router_weight, routes, gate_weight, up_weight,
+    down_weight,
+):
+    count = tokens.shape[0]
+    group = Q_HEADS // KV_HEADS
+    n, m = lax.axis_size("tok"), lax.axis_size("head")
+    head_index = lax.axis_index("head")
+    quarter = down_weight.shape[2]
+    tables = slot_tables(routes, quarter // 128)
+    qkv = project(n, m, tokens, attn_gain, q_weight, k_weight, v_weight)
+    qw, kw = q_weight.shape[1], k_weight.shape[1]
+    kv_local = kw // HD
+    segment = row_request_index[0]
+    positions = row_positions(segment, cache_lengths)
+    queries = rotate(qkv[:, :qw].reshape(count, kv_local * group, HD), positions).astype(BF16)
+    queries = queries.reshape(count, kv_local, group, HD)
+    keys_new = rotate(qkv[:, qw:qw + kw].reshape(count, kv_local, HD), positions).astype(BF16)
+    values_new = qkv[:, qw + kw:].astype(BF16).reshape(count, kv_local, HD)
+    attn = attend(queries, keys_new, values_new, key_cache, value_cache, segment, cache_lengths)
+    cut = functools.partial(lax.dynamic_slice_in_dim, start_index=head_index * quarter, slice_size=quarter)
+    router = jnp.pad(cut(router_weight, axis=0), ((0, 0), (0, 128 - EXPERTS)))
+    return experts(
+        n, m, attn, output_matrix, cut(tokens, axis=1), cut(ffn_gain, axis=0).reshape(1, -1), router,
+        tables, routes, gate_weight, up_weight, down_weight,
+    )
+
+
 def solution(mesh):
     in_specs = (
         P("tok", None),
@@ -180,4 +694,5 @@
         P("tok", None, "head"),
     )
     out_specs = P("tok", "head")
-    return jax.shard_map(shards, mesh=mesh, in_specs=in_specs, out_specs=out_specs, check_vma=False)
+    body = shards_eight if mesh.shape["tok"] == EXPERTS and mesh.shape["head"] == KV_HEADS else shards
+    return jax.shard_map(body, mesh=mesh, in_specs=in_specs, out_specs=out_specs, check_vma=False)

time: 442 us -> 136 us (0.31)
  waiting for transfers between devices: 308 us -> 0 us
  Pallas kernels: 0 us -> 119 us
  matrix products: 52.4 us -> 1.17 us
  blocking collectives: 41.9 us -> 0 us
  between operations: 13.8 us -> 0.25 us
  starting transfers between devices: 5.74 us -> 0 us
    all_gather x5 -> x0, waiting for transfers between devices: 259 us -> none  [the longest x1 72.5 us: shards(): lax.all_gather(q_weight, 'tok', axis=0, tiled=True)]
    pallas_call x0 -> x2, Pallas kernels: none -> 119 us  [the longest x1 88.3 us: experts(): pl.pallas_call(functools.partial(experts_kernel, n, m), out_shape=jax.Sha...]
    dot_general x8 -> x0, matrix products: 51.2 us -> none  [the longest x1 14.7 us: shards(): jnp.einsum('tcf,fd->tcd', hidden_all, down_weight[0], preferred_element_t...]
    all_to_all x1 -> x0, blocking collectives: 41.9 us -> none  [shards(): lax.all_to_all(outgoing, 'tok', split_axis=0, concat_axis=0, tiled=True)]
    psum x1 -> x0, waiting for transfers between devices: 34.1 us -> none  [shards(): mixed = lax.psum(partial_mix, 'head')]
    all_to_all x1 -> x0, waiting for transfers between devices: 11.7 us -> none  [shards(): lax.all_to_all(layer_results, 'tok', split_axis=0, concat_axis=0, tiled=T...]
    scatter x1 -> x0, local copies, waits for them, and re-layouts: 6.15 us -> none  [fill_slots(): jnp.zeros((EXPERTS * CAP, normed_rows.shape[1]), jnp.bfloat16).at[places]]
    all_to_all x1 -> x0, starting transfers between devices: 5.52 us -> none  [shards(): lax.all_to_all(layer_results, 'tok', split_axis=0, concat_axis=0, tiled=T...]
  transfers between devices with their start and end apart: 7 -> 0, of which waited for: 7 -> 0; matrix products, arithmetic and copies ran while one was open for 4% -> 0% of each run, Pallas kernels for 0% -> 0%
where the time goes in v1:
time: 136 us
  Pallas kernels  119 us (88%)
  local copies, waits for them, and re-layouts  9.15 us (7%)
  other arithmetic  6.85 us (5%)
    pallas_call x1, Pallas kernels, experts(): pl.pallas_call(functools.partial(experts_kernel, n, m), out_shape=jax.Sha...  88.3 us
    pallas_call x1, Pallas kernels, project(): pl.pallas_call(functools.partial(project_kernel, n, m), out_shape=jax.Sha...  30.4 us

profile of v1, /device:TPU:0, one launch (start us, length us, event | category | flops | bytes accessed | tf_op | source)
XLA Modules:
  0.0 136.1 jit_solution(14705841203079315887)
XLA Ops:
  0.0 0.8 select_reduce_fusion.1
  0.8 0.9 convert_reduce_fusion
  1.8 0.2 multiply_cosine_fusion
  2.0 30.4 %shard_map.172 = f32[64,768]{1,0:T(8,128)} custom-call(bf16[64,4096]{1,0:T(8,128)(2,1)} %tok_ref.1, f32[1,4096]{1,0:T(1,128)} %bitcast.92, bf16[512,512]{1,0:T(8,128)(2,1)} %q_ref.1, bf16[512,128]{1,0:T(8,128)(2,1)} %k_ref.1, bf16[512,128]{1,0:T(8,128)(2,1)} %v_ref.1), custom_call_target="tpu_custom_call" | custom-call | tf_op jit(solution)/shard_map/pallas_call | solution.py:296
  32.3 0.8 slice_bitcast_fusion.1
  33.2 0.9 pad_maximum_fusion
  34.1 0.9 slice.38
  35.4 0.2 compare_and_fusion
  35.7 0.6 fusion.36
  36.4 0.5 fusion.2
  36.9 0.5 fusion.3
  37.5 0.6 copy.69
  38.4 0.2 reduce_window_sum.11
  38.6 0.2 select_reduce_fusion
  39.0 0.7 fusion.35
  39.9 0.2 broadcast_and_fusion
  40.1 0.8 fusion.11.ptail_ref
  40.9 0.8 fusion.10.seltail_ref
  41.7 0.7 copy.44.pmain_ref
  42.6 0.8 pad.4.router_ref
  43.3 1.6 %constant_dynamic-slice_fusion.1.tok_ref = bf16[64,1024]{1,0:T(8,128)(2,1)} fusion(bf16[64,4096]{1,0:T(8,128)(2,1)} %tok_ref.1, s32[]{:T(128)S(6)} %select_n.100), kind=kLoop, calls=%fused_computation.86 | loop fusion | bytes 262148 | tf_op jit(solution)/shard_map/dynamic_slice | solution.py:672
  44.9 1.3 dynamic_slice.10
  46.2 88.3 %shard_map.173 = bf16[64,1024]{1,0:T(8,128)(2,1)} custom-call(bf16[64,512]{1,0:T(8,128)(2,1)} %bitcast.87, bf16[512,512]{1,0:T(8,128)(2,1)} %w_ref.1, bf16[64,1024]{1,0:T(8,128)(2,1)} %constant_dynamic-slice_fusion.1.tok_ref, f32[1,1024]{1,0:T(1,128)} %bitcast.93, bf16[1024,128]{1,0:T(8,128)(2,1)} %pad.4.router_ref, bf16[128,64]{1,0:T(8,128)(2,1)} %copy.44.pmain_ref, ...), custom_call_target="tpu_custom_call" | custom-call | tf_op jit(solution)/shard_map/pallas_call | solution.py:591
  134.5 1.6 %copy.71 = bf16[64,1024]{1,0:T(8,128)(2,1)} copy(bf16[64,1024]{1,0:T(8,128)(2,1)} %shard_map.173) | data formatting | bytes 262144
  (42 shorter events, 1.5 us)
Async XLA Ops:
  0.0 42.4 %copy-start = (bf16[4096,8]{0,1:T(8,128)(2,1)S(1)}, bf16[4096,8]{0,1:T(8,128)(2,1)}, u32[]{:S(2)}) copy-start(bf16[4096,8]{0,1:T(8,128)(2,1)} %param.29) | copy-start | bytes 196612
  0.0 35.4 %copy-start.4 = (s32[1,64]{1,0:T(1,128)S(1)}, s32[1,64]{1,0:T(1,128)}, u32[]{:S(2)}) copy-start(s32[1,64]{1,0:T(1,128)} %param.27) | copy-start | bytes 772
  0.0 35.7 %copy-start.6 = (bf16[8,256,128]{2,1,0:T(8,128)(2,1)S(1)}, bf16[8,256,128]{2,1,0:T(8,128)(2,1)}, u32[]{:S(2)}) copy-start(bf16[8,256,128]{2,1,0:T(8,128)(2,1)} %param.24) | copy-start | bytes 1572868
  32.3 3.4 %copy-start.2 = (f32[64,768]{1,0:T(8,128)S(1)}, f32[64,768]{1,0:T(8,128)}, u32[]{:S(2)}) copy-start(f32[64,768]{1,0:T(8,128)} %shard_map.172) | copy-start | bytes 589828
  35.7 1.1 copy-start.7
  36.8 1.2 copy-start.5
  38.2 8.0 %copy-start.3 = (s32[64,2]{1,0:T(8,128)}, s32[64,2]{1,0:T(8,128)S(1)}, u32[]{:S(2)}) copy-start(s32[64,2]{1,0:T(8,128)S(1)} %copy.40.chosen_ref) | copy-start | bytes 1540
  46.2 89.9 %copy-start.1 = (bf16[4096,8]{0,1:T(8,128)(2,1)S(1)}, bf16[4096,8]{0,1:T(8,128)(2,1)}, u32[]{:S(2)}) copy-start(bf16[4096,8]{0,1:T(8,128)(2,1)} %param.29) | copy-start | bytes 196612
